TPU v7x, 32 devices: a whole 2x2x4 slice. The times are simulated.
32 devices in a mesh: sub: 4 (over z), wide: 8 (over y, x, core).
Axes of the slice: x: 2, y: 2, z: 4, core: 2. Of those that a mesh axis runs over, the one named last changes fastest.
Arguments:
- load_table: bfloat16 [4, 8, 16, 4, 128], P('sub', 'wide'), may hold values from -6 to 6
- load_column: int32 [64], replicated, may hold values from 0 to 15
- face_order: int32 [4, 8, 4], P('sub', 'wide'), may hold values from 0 to 3, each once within a row
- schur: bfloat16 [4, 8, 512, 512], P('sub', 'wide'), as said below
- neumann: bfloat16 [4, 8, 512, 512], P('sub', 'wide'), as said below
- coarse_basis: bfloat16 [4, 8, 4, 4, 128], P('sub', 'wide'), may hold values from -0.625 to 0.625
- corner_map: int32 [4, 8, 4], P('sub', 'wide'), may hold values from 0 to 47, as said below
- coarse_inverse: float32 [48, 48], P('wide'), as said below
Outputs:
- solution: float32 [4, 8, 4, 64, 128], P('sub', 'wide')
Inputs may be any that keep to these rules, and one draw needn't show every extreme that they name: `corner_map`: each subdomain's 4 entries are distinct; subdomains that meet at a corner of the grid of subdomains give it the same number, and different corners get different numbers, so (5) * (9) of the 48 numbers occur and the others belong to no corner. `coarse_inverse`: Symmetric. `schur`: Symmetric. `neumann`: Symmetric.
All inputs are finite; a program needn't handle non-finite values.
Results may differ from a plain program's by a relative error of at most 0.0014.
Values sent between devices are 32-bit elements; how exact they have to be, the bound alone decides.
A program may use at most 64 MiB of HBM per device.

v0:
```python
import jax
import jax.numpy as jnp
from jax import lax
from jax.sharding import PartitionSpec as P

ITERS = 3


damping = 0.3


def with_halo(cells, sides, width):
    for axis, dim in sides:
        count = lax.axis_size(axis)
        ends = count - 1
        head = lax.slice_in_dim(cells, 0, width, axis=dim)
        tail = lax.slice_in_dim(cells, cells.shape[dim] - width, cells.shape[dim], axis=dim)
        cells = jnp.concatenate(
            [
                lax.ppermute(tail, axis, [(i, (i + 1) % count) for i in range(ends)]),
                cells,
                lax.ppermute(head, axis, [((i + 1) % count, i) for i in range(ends)]),
            ],
            axis=dim,
        )
    return cells


def apply_local(vectors, operators, selector_half, selector_full):
    amount = vectors.shape[0]
    rhs_count = vectors.shape[3]
    face_width = vectors.shape[4]
    rounded = vectors.astype(jnp.bfloat16)
    blocked = jnp.einsum(
        "kcbf,kcfjn->kcjbn", selector_half, rounded, preferred_element_type=jnp.float32
    )
    blocked = blocked.astype(jnp.bfloat16).reshape(amount, 1, rhs_count, 4 * face_width)
    product = jnp.einsum("kcjm,kcmn->kcjn", blocked, operators, preferred_element_type=jnp.float32)
    product = product.reshape(amount, 1, rhs_count, 4, face_width)
    return jnp.einsum("kcbf,kcjbn->kcfjn", selector_full, product, precision=lax.Precision.HIGHEST)


def assemble(copies):
    side_stack = jnp.stack([copies[:, 0, 2], copies[:, 0, 3]], axis=0)
    side_halo = with_halo(side_stack, (("wide", 0),), 1)
    end_stack = jnp.stack([copies[0, 0, 0], copies[-1, 0, 1]], axis=0)
    end_halo = with_halo(end_stack, (("sub", 0),), 1)
    upper_faces = jnp.concatenate([end_halo[0:1], copies[:-1, 0, 1]], axis=0)
    lower_faces = jnp.concatenate([copies[1:, 0, 0], end_halo[3:4]], axis=0)
    north_sum = copies[:, 0, 0] + upper_faces
    south_sum = copies[:, 0, 1] + lower_faces
    west_sum = copies[:, 0, 2] + side_halo[0]
    east_sum = copies[:, 0, 3] + side_halo[3]
    return jnp.stack([north_sum, south_sum, west_sum, east_sum], axis=1)[:, None]


def coarse_solve(partial_value, coarse_inverse):
    assembled = lax.psum(partial_value, ("sub", "wide"))
    owned_rows = jnp.dot(assembled, coarse_inverse.T, precision=lax.Precision.HIGHEST)
    return lax.all_gather(owned_rows, "wide", axis=1, tiled=True)


def body(
    load_table, load_column, face_order, schur, neumann, coarse_basis, corner_map, coarse_inverse
):
    amount = schur.shape[0]
    pattern_count = load_table.shape[2]
    coarse_order = coarse_inverse.shape[1]
    selector_full = (face_order[..., :, None] == jnp.arange(4, dtype=jnp.int32)).astype(jnp.float32)
    selector_half = selector_full.astype(jnp.bfloat16)
    load_select = (load_column[:, None] == jnp.arange(pattern_count, dtype=jnp.int32)).astype(
        jnp.bfloat16
    )
    load_faces = jnp.einsum(
        "jl,kclfn->kcfjn", load_select, load_table, preferred_element_type=jnp.float32
    )
    row_ids = lax.axis_index("sub") * amount + jnp.arange(amount, dtype=jnp.int32)
    rows_total = amount * lax.axis_size("sub")
    column_index = lax.axis_index("wide") * jnp.ones((amount,), jnp.int32)
    cols_total = lax.axis_size("wide")
    half = jnp.float32(0.5)
    whole = jnp.float32(1.0)
    weights = jnp.stack(
        [
            jnp.where(row_ids > 0, half, whole),
            jnp.where(row_ids < rows_total - 1, half, whole),
            jnp.where(column_index > 0, half, whole),
            jnp.where(column_index < cols_total - 1, half, whole),
        ],
        axis=1,
    )[:, None, :, None, None]
    basis = coarse_basis.astype(jnp.float32)
    corner_marks = (corner_map[..., None] == jnp.arange(coarse_order, dtype=jnp.int32)).astype(
        jnp.float32
    )
    solution = jnp.zeros(load_faces.shape, jnp.float32)
    for iteration in range(ITERS):
        if iteration == 0:
            residual = assemble(load_faces)
        else:
            residual = assemble(
                load_faces - apply_local(solution, schur, selector_half, selector_full)
            )
        weighted = weights * residual
        restricted = jnp.einsum(
            "kcpfn,kcfjn->kcpj", basis, weighted, precision=lax.Precision.HIGHEST
        )
        partial_value = jnp.einsum(
            "kcpj,kcpg->jg", restricted, corner_marks, precision=lax.Precision.HIGHEST
        )
        neumann_part = apply_local(weighted, neumann, selector_half, selector_full)
        solved = coarse_solve(partial_value, coarse_inverse)
        picked = jnp.einsum("jg,kcpg->kcpj", solved, corner_marks, precision=lax.Precision.HIGHEST)
        correction = jnp.einsum("kcpj,kcpfn->kcfjn", picked, basis, precision=lax.Precision.HIGHEST)
        update = assemble(weights * (neumann_part + correction))
        solution = solution + damping * update
    return solution


def solution(mesh):
    in_specs = (
        P("sub", "wide", None, None, None),
        P(),
        P("sub", "wide", None),
        P("sub", "wide", None, None),
        P("sub", "wide", None, None),
        P("sub", "wide", None, None, None),
        P("sub", "wide", None),
        P("wide", None),
    )
    out_specs = P("sub", "wide", None, None, None)
    return jax.shard_map(body, mesh=mesh, in_specs=in_specs, out_specs=out_specs, check_vma=False)
```

profile of v0, /device:TPU:0, one launch (start us, length us, event | category | flops | bytes accessed | tf_op | source)
XLA Modules:
  0.0 248.3 jit_solution(4208679977386832550)
XLA Ops:
  0.9 5.0 %collective-permute-start = (f32[1,64,128]{2,1,0:T(8,128)S(1)}, f32[1,64,128]{2,1,0:T(8,128)S(1)}, u32[]{:S(2)}, u32[]{:S(2)}) collective-permute-start(f32[1,64,128]{2,1,0:T(8,128)S(1)} %get-tuple-element.47), channel_id=1, source_target_pairs={{0,8},{8,16},{16,24},{1,9},{9,17},{17,25},{2,10},{10,18},{18,26},{... | collective-permute-start | bytes 98312 | tf_op jit(solution)/shard_map/ppermute | solution.py:20
  5.9 1.5 collective-permute-start.2
  7.4 1.3 collective-permute-start.3
  8.7 1.3 collective-permute-start.1
  12.1 2.4 collective-permute-done.1
  17.3 43.4 %psum.21 = f32[64,48]{0,1:T(8,128)S(1)} all-reduce(f32[64,48]{0,1:T(8,128)S(1)} %fusion.44), channel_id=1, replica_groups=mesh['sub'=4,'wide'=8] {'sub','wide'}, use_global_device_ids=true, to_apply=%region_0.1 | all-reduce | flops 3072 | bytes 24576 | tf_op jit(solution)/shard_map/psum | solution.py:58
  60.9 9.9 %all-gather = f32[8,6,64]{2,1,0:T(8,128)S(1)} all-gather(f32[1,6,64]{2,1,0:T(8,128)S(1)} %convolution_bitcast_fusion.6), channel_id=1, replica_groups=mesh['sub'=4,'wide'=8] {'wide'}, dimensions={0}, use_global_device_ids=true | all-gather | bytes 13824 | tf_op jit(solution)/shard_map/all_gather | solution.py:60
  71.9 2.3 collective-permute-start.6
  74.2 1.3 collective-permute-start.7
  75.7 2.2 collective-permute-start.4
  77.9 1.3 collective-permute-start.5
  79.4 4.2 %collective-permute-done.5 = f32[1,64,128]{2,1,0:T(8,128)S(1)} collective-permute-done((f32[1,64,128]{2,1,0:T(8,128)S(1)}, f32[1,64,128]{2,1,0:T(8,128)S(1)}, u32[]{:S(2)}, u32[]{:S(2)}) %collective-permute-start.5) | collective-permute-done | bytes 32800 | tf_op jit(solution)/shard_map/ppermute | solution.py:22
  84.6 2.3 collective-permute-start.10
  87.0 1.3 collective-permute-start.11
  88.3 3.3 %collective-permute-start.8 = (f32[1,64,128]{2,1,0:T(8,128)S(1)}, f32[1,64,128]{2,1,0:T(8,128)S(1)}, u32[]{:S(2)}, u32[]{:S(2)}) collective-permute-start(f32[1,64,128]{2,1,0:T(8,128)S(1)} %get-tuple-element.31), channel_id=1, source_target_pairs={{0,8},{8,16},{16,24},{1,9},{9,17},{17,25},{2,10},{10,18},{18,26},{... | collective-permute-start | bytes 98312 | tf_op jit(solution)/shard_map/ppermute | solution.py:20
  91.6 1.3 collective-permute-start.9
  93.2 4.2 %collective-permute-done.9 = f32[1,64,128]{2,1,0:T(8,128)S(1)} collective-permute-done((f32[1,64,128]{2,1,0:T(8,128)S(1)}, f32[1,64,128]{2,1,0:T(8,128)S(1)}, u32[]{:S(2)}, u32[]{:S(2)}) %collective-permute-start.9) | collective-permute-done | bytes 32800 | tf_op jit(solution)/shard_map/ppermute | solution.py:22
  98.3 44.9 %psum.22 = f32[64,48]{0,1:T(8,128)S(1)} all-reduce(f32[64,48]{0,1:T(8,128)S(1)} %fusion.43), channel_id=1, replica_groups=mesh['sub'=4,'wide'=8] {'sub','wide'}, use_global_device_ids=true, to_apply=%region_1.2 | all-reduce | flops 3072 | bytes 24576 | tf_op jit(solution)/shard_map/psum | solution.py:58
  143.4 9.9 %all-gather.1 = f32[8,6,64]{2,1,0:T(8,128)S(1)} all-gather(f32[1,6,64]{2,1,0:T(8,128)S(1)} %convolution_bitcast_fusion.5), channel_id=1, replica_groups=mesh['sub'=4,'wide'=8] {'wide'}, dimensions={0}, use_global_device_ids=true | all-gather | bytes 13824 | tf_op jit(solution)/shard_map/all_gather | solution.py:60
  154.4 2.2 collective-permute-start.14
  156.6 1.3 collective-permute-start.15
  157.9 1.9 collective-permute-start.12
  161.4 4.2 %collective-permute-done.13 = f32[1,64,128]{2,1,0:T(8,128)S(1)} collective-permute-done((f32[1,64,128]{2,1,0:T(8,128)S(1)}, f32[1,64,128]{2,1,0:T(8,128)S(1)}, u32[]{:S(2)}, u32[]{:S(2)}) %collective-permute-start.13) | collective-permute-done | bytes 32800 | tf_op jit(solution)/shard_map/ppermute | solution.py:22
  166.6 2.9 %collective-permute-start.18 = (f32[1,1,64,128]{3,2,1,0:T(8,128)S(1)}, f32[1,1,64,128]{3,2,1,0:T(8,128)S(1)}, u32[]{:S(2)}, u32[]{:S(2)}) collective-permute-start(f32[1,1,64,128]{3,2,1,0:T(8,128)S(1)} %get-tuple-element.16), channel_id=1, source_target_pairs={{0,1},{1,2},{2,3},{3,4},{4,5},{5,6},{6,7},{8,9},{9,10},{10,11},{11... | collective-permute-start | bytes 98312 | tf_op jit(solution)/shard_map/ppermute | solution.py:20
  169.4 1.3 collective-permute-start.19
  170.7 2.8 %collective-permute-start.16 = (f32[1,64,128]{2,1,0:T(8,128)S(1)}, f32[1,64,128]{2,1,0:T(8,128)S(1)}, u32[]{:S(2)}, u32[]{:S(2)}) collective-permute-start(f32[1,64,128]{2,1,0:T(8,128)S(1)} %get-tuple-element.15), channel_id=1, source_target_pairs={{0,8},{8,16},{16,24},{1,9},{9,17},{17,25},{2,10},{10,18},{18,26},{... | collective-permute-start | bytes 98312 | tf_op jit(solution)/shard_map/ppermute | solution.py:20
  175.2 4.2 %collective-permute-done.17 = f32[1,64,128]{2,1,0:T(8,128)S(1)} collective-permute-done((f32[1,64,128]{2,1,0:T(8,128)S(1)}, f32[1,64,128]{2,1,0:T(8,128)S(1)}, u32[]{:S(2)}, u32[]{:S(2)}) %collective-permute-start.17) | collective-permute-done | bytes 32800 | tf_op jit(solution)/shard_map/ppermute | solution.py:22
  180.9 44.9 %psum.23 = f32[64,48]{0,1:T(8,128)S(1)} all-reduce(f32[64,48]{0,1:T(8,128)S(1)} %fusion.42), channel_id=1, replica_groups=mesh['sub'=4,'wide'=8] {'sub','wide'}, use_global_device_ids=true, to_apply=%region_2.3 | all-reduce | flops 3072 | bytes 24576 | tf_op jit(solution)/shard_map/psum | solution.py:58
  225.9 9.9 %all-gather.2 = f32[8,6,64]{2,1,0:T(8,128)S(1)} all-gather(f32[1,6,64]{2,1,0:T(8,128)S(1)} %convolution_bitcast_fusion.4), channel_id=1, replica_groups=mesh['sub'=4,'wide'=8] {'wide'}, dimensions={0}, use_global_device_ids=true | all-gather | bytes 13824 | tf_op jit(solution)/shard_map/all_gather | solution.py:60
  236.3 2.2 collective-permute-start.22
  239.9 1.9 collective-permute-start.20
  243.3 4.2 %collective-permute-done.21 = f32[1,64,128]{2,1,0:T(8,128)S(1)} collective-permute-done((f32[1,64,128]{2,1,0:T(8,128)S(1)}, f32[1,64,128]{2,1,0:T(8,128)S(1)}, u32[]{:S(2)}, u32[]{:S(2)}) %collective-permute-start.21) | collective-permute-done | bytes 32800 | tf_op jit(solution)/shard_map/ppermute | solution.py:22
  (104 shorter events, 20.4 us)
Async XLA Ops:
  0.0 0.7 copy-start
  0.0 0.7 copy-start.5
  0.9 11.1 %collective-permute-start = (f32[1,64,128]{2,1,0:T(8,128)S(1)}, f32[1,64,128]{2,1,0:T(8,128)S(1)}, u32[]{:S(2)}, u32[]{:S(2)}) collective-permute-start(f32[1,64,128]{2,1,0:T(8,128)S(1)} %get-tuple-element.47), channel_id=1, source_target_pairs={{0,8},{8,16},{16,24},{1,9},{9,17},{17,25},{2,10},{10,18},{18,26},{... | collective-permute-start | bytes 98312 | tf_op jit(solution)/shard_map/ppermute | solution.py:20
  5.9 5.4 %collective-permute-start.2 = (f32[1,1,64,128]{3,2,1,0:T(8,128)S(1)}, f32[1,1,64,128]{3,2,1,0:T(8,128)S(1)}, u32[]{:S(2)}, u32[]{:S(2)}) collective-permute-start(f32[1,1,64,128]{3,2,1,0:T(8,128)S(1)} %get-tuple-element.48), channel_id=1, source_target_pairs={{0,1},{1,2},{2,3},{3,4},{4,5},{5,6},{6,7},{8,9},{9,10},{10,11},{11... | collective-permute-start | bytes 98312 | tf_op jit(solution)/shard_map/ppermute | solution.py:20
  7.4 4.7 %collective-permute-start.3 = (f32[1,1,64,128]{3,2,1,0:T(8,128)S(1)}, f32[1,1,64,128]{3,2,1,0:T(8,128)S(1)}, u32[]{:S(2)}, u32[]{:S(2)}) collective-permute-start(f32[1,1,64,128]{3,2,1,0:T(8,128)S(1)} %get-tuple-element.49), channel_id=1, source_target_pairs={{1,0},{2,1},{3,2},{4,3},{5,4},{6,5},{7,6},{9,8},{10,9},{11,10},{12... | collective-permute-start | bytes 98312 | tf_op jit(solution)/shard_map/ppermute | solution.py:22
  8.7 5.8 %collective-permute-start.1 = (f32[1,64,128]{2,1,0:T(8,128)S(1)}, f32[1,64,128]{2,1,0:T(8,128)S(1)}, u32[]{:S(2)}, u32[]{:S(2)}) collective-permute-start(f32[1,64,128]{2,1,0:T(8,128)S(1)} %get-tuple-element.50), channel_id=1, source_target_pairs={{8,0},{16,8},{24,16},{9,1},{17,9},{25,17},{10,2},{18,10},{26,18},{... | collective-permute-start | bytes 98312 | tf_op jit(solution)/shard_map/ppermute | solution.py:22
  14.5 0.7 copy-start.2
  15.4 0.7 copy-start.4
  16.4 0.7 copy-start.6
  17.3 43.5 %copy-start.3 = (f32[6,48]{1,0:T(8,128)S(1)}, f32[6,48]{1,0:T(8,128)}, u32[]{:S(2)}) copy-start(f32[6,48]{1,0:T(8,128)} %param.15) | copy-start | bytes 3460
  71.3 4.2 %copy-start.1 = (bf16[1,1,512,512]{3,2,1,0:T(8,128)(2,1)S(1)}, bf16[1,1,512,512]{3,2,1,0:T(8,128)(2,1)}, u32[]{:S(2)}) copy-start(bf16[1,1,512,512]{3,2,1,0:T(8,128)(2,1)} %param.11) | copy-start | bytes 1572868
  71.9 7.2 %collective-permute-start.6 = (f32[1,1,64,128]{3,2,1,0:T(8,128)S(1)}, f32[1,1,64,128]{3,2,1,0:T(8,128)S(1)}, u32[]{:S(2)}, u32[]{:S(2)}) collective-permute-start(f32[1,1,64,128]{3,2,1,0:T(8,128)S(1)} %get-tuple-element.40), channel_id=1, source_target_pairs={{0,1},{1,2},{2,3},{3,4},{4,5},{5,6},{6,7},{8,9},{9,10},{10,11},{11... | collective-permute-start | bytes 98312 | tf_op jit(solution)/shard_map/ppermute | solution.py:20
  74.2 5.0 %collective-permute-start.7 = (f32[1,1,64,128]{3,2,1,0:T(8,128)S(1)}, f32[1,1,64,128]{3,2,1,0:T(8,128)S(1)}, u32[]{:S(2)}, u32[]{:S(2)}) collective-permute-start(f32[1,1,64,128]{3,2,1,0:T(8,128)S(1)} %get-tuple-element.41), channel_id=1, source_target_pairs={{1,0},{2,1},{3,2},{4,3},{5,4},{6,5},{7,6},{9,8},{10,9},{11,10},{12... | collective-permute-start | bytes 98312 | tf_op jit(solution)/shard_map/ppermute | solution.py:22
  75.7 3.7 %collective-permute-start.4 = (f32[1,64,128]{2,1,0:T(8,128)S(1)}, f32[1,64,128]{2,1,0:T(8,128)S(1)}, u32[]{:S(2)}, u32[]{:S(2)}) collective-permute-start(f32[1,64,128]{2,1,0:T(8,128)S(1)} %get-tuple-element.39), channel_id=1, source_target_pairs={{0,8},{8,16},{16,24},{1,9},{9,17},{17,25},{2,10},{10,18},{18,26},{... | collective-permute-start | bytes 98312 | tf_op jit(solution)/shard_map/ppermute | solution.py:20
  77.9 5.8 %collective-permute-start.5 = (f32[1,64,128]{2,1,0:T(8,128)S(1)}, f32[1,64,128]{2,1,0:T(8,128)S(1)}, u32[]{:S(2)}, u32[]{:S(2)}) collective-permute-start(f32[1,64,128]{2,1,0:T(8,128)S(1)} %get-tuple-element.42), channel_id=1, source_target_pairs={{8,0},{16,8},{24,16},{9,1},{17,9},{25,17},{10,2},{18,10},{26,18},{... | collective-permute-start | bytes 98312 | tf_op jit(solution)/shard_map/ppermute | solution.py:22
  84.6 8.3 %collective-permute-start.10 = (f32[1,1,64,128]{3,2,1,0:T(8,128)S(1)}, f32[1,1,64,128]{3,2,1,0:T(8,128)S(1)}, u32[]{:S(2)}, u32[]{:S(2)}) collective-permute-start(f32[1,1,64,128]{3,2,1,0:T(8,128)S(1)} %get-tuple-element.32), channel_id=1, source_target_pairs={{0,1},{1,2},{2,3},{3,4},{4,5},{5,6},{6,7},{8,9},{9,10},{10,11},{11... | collective-permute-start | bytes 98312 | tf_op jit(solution)/shard_map/ppermute | solution.py:20
  87.0 6.0 %collective-permute-start.11 = (f32[1,1,64,128]{3,2,1,0:T(8,128)S(1)}, f32[1,1,64,128]{3,2,1,0:T(8,128)S(1)}, u32[]{:S(2)}, u32[]{:S(2)}) collective-permute-start(f32[1,1,64,128]{3,2,1,0:T(8,128)S(1)} %get-tuple-element.33), channel_id=1, source_target_pairs={{1,0},{2,1},{3,2},{4,3},{5,4},{6,5},{7,6},{9,8},{10,9},{11,10},{12... | collective-permute-start | bytes 98312 | tf_op jit(solution)/shard_map/ppermute | solution.py:22
  88.3 4.9 %collective-permute-start.8 = (f32[1,64,128]{2,1,0:T(8,128)S(1)}, f32[1,64,128]{2,1,0:T(8,128)S(1)}, u32[]{:S(2)}, u32[]{:S(2)}) collective-permute-start(f32[1,64,128]{2,1,0:T(8,128)S(1)} %get-tuple-element.31), channel_id=1, source_target_pairs={{0,8},{8,16},{16,24},{1,9},{9,17},{17,25},{2,10},{10,18},{18,26},{... | collective-permute-start | bytes 98312 | tf_op jit(solution)/shard_map/ppermute | solution.py:20
  91.6 5.8 %collective-permute-start.9 = (f32[1,64,128]{2,1,0:T(8,128)S(1)}, f32[1,64,128]{2,1,0:T(8,128)S(1)}, u32[]{:S(2)}, u32[]{:S(2)}) collective-permute-start(f32[1,64,128]{2,1,0:T(8,128)S(1)} %get-tuple-element.34), channel_id=1, source_target_pairs={{8,0},{16,8},{24,16},{9,1},{17,9},{25,17},{10,2},{18,10},{26,18},{... | collective-permute-start | bytes 98312 | tf_op jit(solution)/shard_map/ppermute | solution.py:22
  154.4 6.7 %collective-permute-start.14 = (f32[1,1,64,128]{3,2,1,0:T(8,128)S(1)}, f32[1,1,64,128]{3,2,1,0:T(8,128)S(1)}, u32[]{:S(2)}, u32[]{:S(2)}) collective-permute-start(f32[1,1,64,128]{3,2,1,0:T(8,128)S(1)} %get-tuple-element.24), channel_id=1, source_target_pairs={{0,1},{1,2},{2,3},{3,4},{4,5},{5,6},{6,7},{8,9},{9,10},{10,11},{11... | collective-permute-start | bytes 98312 | tf_op jit(solution)/shard_map/ppermute | solution.py:20
  156.6 4.5 %collective-permute-start.15 = (f32[1,1,64,128]{3,2,1,0:T(8,128)S(1)}, f32[1,1,64,128]{3,2,1,0:T(8,128)S(1)}, u32[]{:S(2)}, u32[]{:S(2)}) collective-permute-start(f32[1,1,64,128]{3,2,1,0:T(8,128)S(1)} %get-tuple-element.25), channel_id=1, source_target_pairs={{1,0},{2,1},{3,2},{4,3},{5,4},{6,5},{7,6},{9,8},{10,9},{11,10},{12... | collective-permute-start | bytes 98312 | tf_op jit(solution)/shard_map/ppermute | solution.py:22
  157.9 3.4 %collective-permute-start.12 = (f32[1,64,128]{2,1,0:T(8,128)S(1)}, f32[1,64,128]{2,1,0:T(8,128)S(1)}, u32[]{:S(2)}, u32[]{:S(2)}) collective-permute-start(f32[1,64,128]{2,1,0:T(8,128)S(1)} %get-tuple-element.23), channel_id=1, source_target_pairs={{0,8},{8,16},{16,24},{1,9},{9,17},{17,25},{2,10},{10,18},{18,26},{... | collective-permute-start | bytes 98312 | tf_op jit(solution)/shard_map/ppermute | solution.py:20
  159.8 5.8 %collective-permute-start.13 = (f32[1,64,128]{2,1,0:T(8,128)S(1)}, f32[1,64,128]{2,1,0:T(8,128)S(1)}, u32[]{:S(2)}, u32[]{:S(2)}) collective-permute-start(f32[1,64,128]{2,1,0:T(8,128)S(1)} %get-tuple-element.26), channel_id=1, source_target_pairs={{8,0},{16,8},{24,16},{9,1},{17,9},{25,17},{10,2},{18,10},{26,18},{... | collective-permute-start | bytes 98312 | tf_op jit(solution)/shard_map/ppermute | solution.py:22
  166.6 8.3 %collective-permute-start.18 = (f32[1,1,64,128]{3,2,1,0:T(8,128)S(1)}, f32[1,1,64,128]{3,2,1,0:T(8,128)S(1)}, u32[]{:S(2)}, u32[]{:S(2)}) collective-permute-start(f32[1,1,64,128]{3,2,1,0:T(8,128)S(1)} %get-tuple-element.16), channel_id=1, source_target_pairs={{0,1},{1,2},{2,3},{3,4},{4,5},{5,6},{6,7},{8,9},{9,10},{10,11},{11... | collective-permute-start | bytes 98312 | tf_op jit(solution)/shard_map/ppermute | solution.py:20
  169.4 5.8 %collective-permute-start.19 = (f32[1,1,64,128]{3,2,1,0:T(8,128)S(1)}, f32[1,1,64,128]{3,2,1,0:T(8,128)S(1)}, u32[]{:S(2)}, u32[]{:S(2)}) collective-permute-start(f32[1,1,64,128]{3,2,1,0:T(8,128)S(1)} %get-tuple-element.17), channel_id=1, source_target_pairs={{1,0},{2,1},{3,2},{4,3},{5,4},{6,5},{7,6},{9,8},{10,9},{11,10},{12... | collective-permute-start | bytes 98312 | tf_op jit(solution)/shard_map/ppermute | solution.py:22
  170.7 4.5 %collective-permute-start.16 = (f32[1,64,128]{2,1,0:T(8,128)S(1)}, f32[1,64,128]{2,1,0:T(8,128)S(1)}, u32[]{:S(2)}, u32[]{:S(2)}) collective-permute-start(f32[1,64,128]{2,1,0:T(8,128)S(1)} %get-tuple-element.15), channel_id=1, source_target_pairs={{0,8},{8,16},{16,24},{1,9},{9,17},{17,25},{2,10},{10,18},{18,26},{... | collective-permute-start | bytes 98312 | tf_op jit(solution)/shard_map/ppermute | solution.py:20
  173.6 5.8 %collective-permute-start.17 = (f32[1,64,128]{2,1,0:T(8,128)S(1)}, f32[1,64,128]{2,1,0:T(8,128)S(1)}, u32[]{:S(2)}, u32[]{:S(2)}) collective-permute-start(f32[1,64,128]{2,1,0:T(8,128)S(1)} %get-tuple-element.18), channel_id=1, source_target_pairs={{8,0},{16,8},{24,16},{9,1},{17,9},{25,17},{10,2},{18,10},{26,18},{... | collective-permute-start | bytes 98312 | tf_op jit(solution)/shard_map/ppermute | solution.py:22
  236.3 6.7 %collective-permute-start.22 = (f32[1,1,64,128]{3,2,1,0:T(8,128)S(1)}, f32[1,1,64,128]{3,2,1,0:T(8,128)S(1)}, u32[]{:S(2)}, u32[]{:S(2)}) collective-permute-start(f32[1,1,64,128]{3,2,1,0:T(8,128)S(1)} %get-tuple-element.8), channel_id=1, source_target_pairs={{0,1},{1,2},{2,3},{3,4},{4,5},{5,6},{6,7},{8,9},{9,10},{10,11},{11... | collective-permute-start | bytes 98312 | tf_op jit(solution)/shard_map/ppermute | solution.py:20
  238.6 4.5 %collective-permute-start.23 = (f32[1,1,64,128]{3,2,1,0:T(8,128)S(1)}, f32[1,1,64,128]{3,2,1,0:T(8,128)S(1)}, u32[]{:S(2)}, u32[]{:S(2)}) collective-permute-start(f32[1,1,64,128]{3,2,1,0:T(8,128)S(1)} %get-tuple-element.9), channel_id=1, source_target_pairs={{1,0},{2,1},{3,2},{4,3},{5,4},{6,5},{7,6},{9,8},{10,9},{11,10},{12... | collective-permute-start | bytes 98312 | tf_op jit(solution)/shard_map/ppermute | solution.py:22
  239.9 3.4 %collective-permute-start.20 = (f32[1,64,128]{2,1,0:T(8,128)S(1)}, f32[1,64,128]{2,1,0:T(8,128)S(1)}, u32[]{:S(2)}, u32[]{:S(2)}) collective-permute-start(f32[1,64,128]{2,1,0:T(8,128)S(1)} %get-tuple-element.7), channel_id=1, source_target_pairs={{0,8},{8,16},{16,24},{1,9},{9,17},{17,25},{2,10},{10,18},{18,26},{... | collective-permute-start | bytes 98312 | tf_op jit(solution)/shard_map/ppermute | solution.py:20
  241.8 5.8 %collective-permute-start.21 = (f32[1,64,128]{2,1,0:T(8,128)S(1)}, f32[1,64,128]{2,1,0:T(8,128)S(1)}, u32[]{:S(2)}, u32[]{:S(2)}) collective-permute-start(f32[1,64,128]{2,1,0:T(8,128)S(1)} %get-tuple-element.10), channel_id=1, source_target_pairs={{8,0},{16,8},{24,16},{9,1},{17,9},{25,17},{10,2},{18,10},{26,18},{... | collective-permute-start | bytes 98312 | tf_op jit(solution)/shard_map/ppermute | solution.py:22
where the time goes:
time: 251 us; the launch traced here: 248 us
  blocking collectives  163 us (65%)
  starting transfers between devices  45.9 us (18%)
  waiting for transfers between devices  25.5 us (10%)
  matrix products  7.57 us (3%)
  local copies, waits for them, and re-layouts  4.4 us (2%)
    psum x3, blocking collectives, coarse_solve(): assembled = lax.psum(partial_value, ('sub', 'wide'))  133 us
    ppermute x12, starting transfers between devices, with_halo(): lax.ppermute(tail, axis, [(i, (i + 1) % count) for i in range(ends)])  30.4 us
    all_gather x3, blocking collectives, coarse_solve(): return lax.all_gather(owned_rows, 'wide', axis=1, tiled=True)  29.7 us
    ppermute x12, waiting for transfers between devices, with_halo(): lax.ppermute(head, axis, [((i + 1) % count, i) for i in range(ends)])  24.5 us
    ppermute x12, starting transfers between devices, with_halo(): lax.ppermute(head, axis, [((i + 1) % count, i) for i in range(ends)])  15.5 us
  transfers between devices with their start and end apart: 24, of which 12 were waited for; matrix products, arithmetic and copies ran while one was open for 1% of the time, Pallas kernels for 0%

commit v1 on v0

v1 whole, which is shorter than its diff:
```python
import functools

import jax
import jax.numpy as jnp
from jax import lax
from jax.experimental import pallas as pl
from jax.experimental.pallas import tpu as pltpu
from jax.sharding import PartitionSpec as P

ITERS = 3
damping = 0.3
MESH = pl.DeviceIdType.MESH
HIGHEST = lax.Precision.HIGHEST
OPPOSITE = (1, 0, 3, 2)


def split(value):
    high = value.astype(jnp.bfloat16)
    low = (value - high.astype(jnp.float32)).astype(jnp.bfloat16)
    return high, low


def dot(a, b, dims, precision=None):
    return lax.dot_general(
        a, b, (dims, ((), ())), precision=precision, preferred_element_type=jnp.float32
    )


def kernel(
    sizes,
    face_order,
    corner_map,
    load_column,
    load_table,
    basis_in,
    inverse_in,
    schur_hbm,
    neumann_hbm,
    out,
    schur,
    neumann,
    load,
    sol,
    face_out,
    face_in,
    basis_out,
    basis_near,
    corner_all,
    corner_flat,
    inverse_all,
    inverse_flat,
    gmat,
    hmat,
    rest_all,
    rest_flat,
    local_sem,
    face_send,
    face_recv,
    basis_send,
    basis_recv,
    corner_send,
    corner_recv,
    inverse_send,
    inverse_recv,
    rest_send,
    rest_recv,
):
    subs, wides = sizes
    devices = subs * wides
    rhs, width = sol.shape[1], sol.shape[2]
    prims = basis_out.shape[1]
    order = inverse_flat.shape[0]
    owned = inverse_in.shape[0]
    row = lax.axis_index("sub")
    col = lax.axis_index("wide")
    me = row * wides + col
    has = (row > 0, row < subs - 1, col > 0, col < wides - 1)
    near = ((row - 1, col), (row + 1, col), (row, col - 1), (row, col + 1))
    share = [jnp.where(flag, jnp.float32(0.5), jnp.float32(1.0)) for flag in has]

    def place(step):
        peer = lax.rem(me + step, devices)
        return peer, (peer // wides, lax.rem(peer, wides))

    def each_peer(action):
        def one(step, carry):
            action(*place(step))
            return carry

        lax.fori_loop(1, devices, one, 0)

    load_n = pltpu.make_async_copy(neumann_hbm, neumann, local_sem.at[0])
    load_s = pltpu.make_async_copy(schur_hbm, schur, local_sem.at[1])
    load_n.start()
    load_s.start()

    barrier = pltpu.get_barrier_semaphore()
    each_peer(
        lambda peer, where: pl.semaphore_signal(
            barrier, inc=1, device_id=where, device_id_type=MESH
        )
    )

    basis = basis_in[...].astype(jnp.float32)
    for f in range(4):
        basis_out[f] = jnp.concatenate(
            [basis[4 * p + f : 4 * p + f + 1] for p in range(prims)], axis=0
        )
    row_of = lax.broadcasted_iota(jnp.int32, (prims, 128), 0)
    marks = jnp.zeros((prims, 128), jnp.int32)
    for p in range(prims):
        marks = jnp.where(row_of == p, corner_map[p], marks)
    corner_all[me] = marks
    table = load_table[...]
    wanted = load_column[...] * 4
    pattern = lax.broadcasted_iota(jnp.int32, (table.shape[0], rhs), 0)
    for f in range(4):
        chosen = (pattern == wanted + f).astype(jnp.float32)
        load[f] = dot(chosen.T.astype(jnp.bfloat16), table, ((1,), (0,)))
        face_out[0, f] = load[f]
    inverse_all[col] = inverse_in[...]
    for f in range(4):

        @pl.when(jnp.logical_not(has[f]))
        def _():
            for turn in range(2 * ITERS):
                face_in[turn, f] = jnp.zeros((rhs, width), jnp.float32)
            basis_near[f] = jnp.zeros((prims, width), jnp.float32)

    pl.semaphore_wait(barrier, devices - 1)

    def face_copy(turn, f):
        return pltpu.make_async_remote_copy(
            src_ref=face_out.at[turn, f],
            dst_ref=face_in.at[turn, OPPOSITE[f]],
            send_sem=face_send.at[turn, f],
            recv_sem=face_recv.at[turn, OPPOSITE[f]],
            device_id=near[f],
            device_id_type=MESH,
        )

    def face_wait(turn, f):
        pltpu.make_async_copy(
            face_out.at[turn, f], face_in.at[turn, f], face_recv.at[turn, f]
        ).wait()

    def basis_copy(f):
        return pltpu.make_async_remote_copy(
            src_ref=basis_out.at[f],
            dst_ref=basis_near.at[OPPOSITE[f]],
            send_sem=basis_send.at[f],
            recv_sem=basis_recv.at[OPPOSITE[f]],
            device_id=near[f],
            device_id_type=MESH,
        )

    def corner_copy(peer, where):
        return pltpu.make_async_remote_copy(
            src_ref=corner_all.at[me],
            dst_ref=corner_all.at[me],
            send_sem=corner_send.at[0],
            recv_sem=corner_recv.at[0],
            device_id=where,
            device_id_type=MESH,
        )

    def inverse_copy(other):
        return pltpu.make_async_remote_copy(
            src_ref=inverse_all.at[col],
            dst_ref=inverse_all.at[col],
            send_sem=inverse_send.at[other],
            recv_sem=inverse_recv.at[col],
            device_id=(row, other),
            device_id_type=MESH,
        )

    def rest_copy(iteration, peer, where):
        return pltpu.make_async_remote_copy(
            src_ref=rest_all.at[iteration, me],
            dst_ref=rest_all.at[iteration, me],
            send_sem=rest_send.at[iteration],
            recv_sem=rest_recv.at[iteration],
            device_id=where,
            device_id_type=MESH,
        )

    def wait_others(blocks, sem):
        others = blocks.at[pl.ds(0, devices - 1)]
        pltpu.make_async_copy(others, others, sem).wait()

    def send_faces(turn):
        for f in (0, 1, 2, 3):

            @pl.when(has[f])
            def _():
                face_copy(turn, f).start()

    def wait_faces(turn):
        for f in (0, 1, 2, 3):

            @pl.when(has[f])
            def _():
                face_wait(turn, f)

    send_faces(0)
    for f in range(4):

        @pl.when(has[f])
        def _():
            basis_copy(f).start()

    each_peer(lambda peer, where: corner_copy(peer, where).start())

    def each_wide(action):
        def one(step, carry):
            action(lax.rem(col + step, wides))
            return carry

        lax.fori_loop(1, wides, one, 0)

    each_wide(lambda other: inverse_copy(other).start())

    order_of = [jnp.full((rhs, width), face_order[b], jnp.int32) for b in range(4)]
    held = [[order_of[b] == f for f in range(4)] for b in range(4)]

    def pick(masks, values):
        chosen = values[3]
        for i in range(3):
            chosen = jnp.where(masks[i], values[i], chosen)
        return chosen

    def apply_local(vectors, operator):
        blocked = jnp.concatenate(
            [pick(held[b], vectors).astype(jnp.bfloat16) for b in range(4)], axis=1
        )
        result = dot(blocked, operator[...], ((1,), (0,)))
        parts = [result[:, b * width : (b + 1) * width] for b in range(4)]
        return [pick([held[b][f] for b in range(4)], parts) for f in range(4)]

    own_basis = jnp.concatenate([basis_out[f] for f in range(4)], axis=1)
    own_half = own_basis.astype(jnp.bfloat16)
    group = min(devices, 32)
    span = group * prims

    def prepare():
        each_wide(
            lambda other: pltpu.make_async_copy(
                inverse_all.at[other], inverse_all.at[other], inverse_recv.at[other]
            ).wait()
        )
        for w in range(wides):
            inverse_flat[w * owned : (w + 1) * owned, :] = inverse_all[w]
        for f in range(4):

            @pl.when(has[f])
            def _():
                pltpu.make_async_copy(
                    basis_near.at[f], basis_near.at[f], basis_recv.at[f]
                ).wait()

        wait_others(corner_all, corner_recv.at[0])
        gmat[...] = jnp.zeros(gmat.shape, jnp.float32)
        gmat[0:prims, :] = own_basis
        for f in range(4):
            gmat[(f + 1) * prims : (f + 2) * prims, f * width : (f + 1) * width] = basis_near[f]
        lanes = lax.broadcasted_iota(jnp.int32, (prims, order), 1)
        picks = [marks[:, :1] == lanes]
        for f in range(4):
            peer = jnp.where(has[f], near[f][0] * wides + near[f][1], me)
            picks.append(corner_all[peer][:, :1] == lanes)
        mine = jnp.concatenate([pick.astype(jnp.float32) for pick in picks], axis=0)
        columns = dot(mine, inverse_flat[...], ((1,), (0,)), HIGHEST)
        spread = dot(columns.T, gmat[0 : 5 * prims, :], ((1,), (0,)), HIGHEST)

        def one(part):
            for d in range(group):
                corner_flat[d * prims : (d + 1) * prims, :] = corner_all[part * group + d]
            wide_lanes = lax.broadcasted_iota(jnp.int32, (span, order), 1)
            chosen = (corner_flat[:, :1] == wide_lanes).astype(jnp.float32)
            hmat[pl.ds(pl.multiple_of(part * span, span), span), :] = dot(
                chosen, spread, ((1,), (0,)), HIGHEST
            )

        if devices == group:
            one(0)
        else:
            lax.fori_loop(0, devices // group, lambda part, carry: (one(part), carry)[1], 0)

    def correct(iteration):
        def one(part):
            for d in range(group):
                rest_flat[d * prims : (d + 1) * prims, :] = rest_all[iteration, part * group + d]
            return dot(
                rest_flat[...].T,
                hmat[pl.ds(pl.multiple_of(part * span, span), span), :],
                ((1,), (0,)),
                HIGHEST,
            )

        if devices == group:
            return one(0)
        return lax.fori_loop(
            0,
            devices // group,
            lambda part, total: total + one(part),
            jnp.zeros((rhs, 4 * width), jnp.float32),
        )

    for iteration in range(ITERS):
        first = 2 * iteration
        if iteration > 0:
            if iteration == 1:
                load_s.wait()
            local = apply_local([sol[f] for f in range(4)], schur)
            for f in range(4):
                face_out[first, f] = load[f] - local[f]
            send_faces(first)
        wait_faces(first)
        weighted = [share[f] * (face_out[first, f] + face_in[first, f]) for f in range(4)]
        high, low = split(jnp.concatenate(weighted, axis=1))
        restricted = dot(own_half, high, ((1,), (1,))) + dot(own_half, low, ((1,), (1,)))
        rest_all[iteration, me] = restricted
        each_peer(lambda peer, where: rest_copy(iteration, peer, where).start())
        if iteration == 0:
            load_n.wait()
        local = apply_local(weighted, neumann)
        for f in range(4):
            face_out[first + 1, f] = local[f]
        send_faces(first + 1)
        if iteration == 0:
            prepare()
        wait_others(rest_all.at[iteration], rest_recv.at[iteration])
        correction = correct(iteration)
        wait_faces(first + 1)
        for f in range(4):
            update = share[f] * (
                face_out[first + 1, f]
                + face_in[first + 1, f]
                + correction[:, f * width : (f + 1) * width]
            )
            if iteration == 0:
                sol[f] = damping * update
            elif iteration < ITERS - 1:
                sol[f] = sol[f] + damping * update
            else:
                out[f] = sol[f] + damping * update

    for turn in range(2 * ITERS):
        for f in range(4):

            @pl.when(has[f])
            def _():
                face_copy(turn, f).wait_send()

    for f in range(4):

        @pl.when(has[f])
        def _():
            basis_copy(f).wait_send()

    each_wide(lambda other: inverse_copy(other).wait_send())

    wait_others(corner_all, corner_send.at[0])
    for iteration in range(ITERS):
        wait_others(rest_all.at[iteration], rest_send.at[iteration])


def body(
    load_table, load_column, face_order, schur, neumann, coarse_basis, corner_map, coarse_inverse
):
    subs, wides = lax.axis_size("sub"), lax.axis_size("wide")
    devices = subs * wides
    patterns, width = load_table.shape[2], load_table.shape[4]
    rhs = load_column.shape[0]
    inner = schur.shape[2]
    prims = coarse_basis.shape[2]
    owned, order = coarse_inverse.shape
    assert schur.shape[0] == 1 and schur.shape[1] == 1
    f32 = jnp.float32
    group = min(devices, 32)
    dma = pltpu.SemaphoreType.DMA
    vmem = pl.BlockSpec(memory_space=pltpu.VMEM)
    smem = pl.BlockSpec(memory_space=pltpu.SMEM)
    hbm = pl.BlockSpec(memory_space=pl.ANY)
    result = pl.pallas_call(
        functools.partial(kernel, (subs, wides)),
        out_shape=jax.ShapeDtypeStruct((4, rhs, width), f32),
        in_specs=[smem, smem, vmem, vmem, vmem, vmem, hbm, hbm],
        out_specs=vmem,
        scratch_shapes=[
            pltpu.VMEM((inner, inner), schur.dtype),
            pltpu.VMEM((inner, inner), neumann.dtype),
            pltpu.VMEM((4, rhs, width), f32),
            pltpu.VMEM((4, rhs, width), f32),
            pltpu.VMEM((2 * ITERS, 4, rhs, width), f32),
            pltpu.VMEM((2 * ITERS, 4, rhs, width), f32),
            pltpu.VMEM((4, prims, width), f32),
            pltpu.VMEM((4, prims, width), f32),
            pltpu.VMEM((devices, prims, 128), jnp.int32),
            pltpu.VMEM((group * prims, 128), jnp.int32),
            pltpu.VMEM((wides, owned, order), f32),
            pltpu.VMEM((order, order), f32),
            pltpu.VMEM((5 * prims, 4 * width), f32),
            pltpu.VMEM((devices * prims, 4 * width), f32),
            pltpu.VMEM((ITERS, devices, prims, rhs), f32),
            pltpu.VMEM((group * prims, rhs), f32),
            dma((2,)),
            dma((2 * ITERS, 4)),
            dma((2 * ITERS, 4)),
            dma((4,)),
            dma((4,)),
            dma((1,)),
            dma((1,)),
            dma((wides,)),
            dma((wides,)),
            dma((ITERS,)),
            dma((ITERS,)),
        ],
        compiler_params=pltpu.CompilerParams(collective_id=0, has_side_effects=True),
        name="bddc",
    )(
        face_order.reshape(4),
        corner_map.reshape(prims),
        load_column.reshape(1, rhs),
        load_table.reshape(patterns * 4, width),
        coarse_basis.reshape(prims * 4, width),
        coarse_inverse,
        schur.reshape(inner, inner),
        neumann.reshape(inner, inner),
    )
    return result.reshape(1, 1, 4, rhs, width)


def solution(mesh):
    in_specs = (
        P("sub", "wide", None, None, None),
        P(),
        P("sub", "wide", None),
        P("sub", "wide", None, None),
        P("sub", "wide", None, None),
        P("sub", "wide", None, None, None),
        P("sub", "wide", None),
        P("wide", None),
    )
    out_specs = P("sub", "wide", None, None, None)
    return jax.shard_map(body, mesh=mesh, in_specs=in_specs, out_specs=out_specs, check_vma=False)
```

time: 251 us -> 34.9 us (0.14); the launches traced: 248 us -> 34.7 us
  blocking collectives: 163 us -> 0 us
  starting transfers between devices: 45.9 us -> 0 us
  Pallas kernels: 0 us -> 33.1 us
  waiting for transfers between devices: 25.5 us -> 0 us
  matrix products: 7.57 us -> 0 us
  local copies, waits for them, and re-layouts: 4.4 us -> 1.57 us
    psum x3 -> x0, blocking collectives: 133 us -> none  [coarse_solve(): assembled = lax.psum(partial_value, ('sub', 'wide'))]
    ppermute x24 -> x0, starting transfers between devices: 45.9 us -> none  [the longest x12 30.4 us: with_halo(): lax.ppermute(tail, axis, [(i, (i + 1) % count) for i in range(ends)])]
    pallas_call x0 -> x1, Pallas kernels: none -> 33.1 us  [body(): pl.pallas_call(functools.partial(kernel, (subs, wides)), out_shape=jax.Sh...]
    all_gather x3 -> x0, blocking collectives: 29.7 us -> none  [coarse_solve(): return lax.all_gather(owned_rows, 'wide', axis=1, tiled=True)]
    ppermute x24 -> x0, waiting for transfers between devices: 25.5 us -> none  [the longest x12 24.5 us: with_halo(): lax.ppermute(head, axis, [((i + 1) % count, i) for i in range(ends)])]
    dot_general x31 -> x0, matrix products: 7.57 us -> none  [the longest x5 1.62 us: apply_local(): jnp.einsum('kcbf,kcjbn->kcfjn', selector_full, product, precision=lax.Pre...]
  transfers between devices with their start and end apart: 24 -> 0, of which waited for: 12 -> 0; matrix products, arithmetic and copies ran while one was open for 1% -> 0% of each run, Pallas kernels for 0% -> 0%
where the time goes in v1:
time: 34.9 us; the launch traced here: 34.7 us
  Pallas kernels  33.1 us (95%)
  local copies, waits for them, and re-layouts  1.57 us (4%)
    pallas_call x1, Pallas kernels, body(): pl.pallas_call(functools.partial(kernel, (subs, wides)), out_shape=jax.Sh...  33.1 us
    unnamed x1, local copies, waits for them, and re-layouts  1.57 us

profile of v1, /device:TPU:0, one launch (start us, length us, event | category | flops | bytes accessed | tf_op | source)
XLA Modules:
  0.0 34.7 jit_solution(6702068638412195647)
XLA Ops:
  0.0 33.1 %bddc.1 = f32[4,64,128]{2,1,0:T(8,128)} custom-call(s32[4]{0:T(128)} %bitcast.13, s32[4]{0:T(128)} %bitcast.14, s32[1,64]{1,0:T(1,128)} %bitcast.15, bf16[64,128]{1,0:T(8,128)(2,1)} %bitcast.11, bf16[16,128]{1,0:T(8,128)(2,1)} %bitcast.12, f32[6,48]{1,0:T(8,128)} %inverse_in.1, bf16[512,512]{1,0:T(8,128)(2,1)} %bitcast.8, bf16[512,512]{1,0:T(8,128)(2,1)} %bitcast.9), custom_call_target="tpu_custom_call" | custom-call | tf_op jit(solution)/shard_map/bddc/pallas_call | solution.py:385
  33.1 1.6 %copy.10 = f32[1,1,4,64,128]{4,3,2,1,0:T(8,128)} copy(f32[1,1,4,64,128]{4,3,2,1,0:T(8,128)} %bitcast.10) | data formatting | bytes 262144

commit v2 on v1

--- a/solution.py
+++ b/solution.py
@@ -30,7 +30,6 @@
     sizes,
     face_order,
     corner_map,
-    load_column,
     load_table,
     basis_in,
     inverse_in,
@@ -50,9 +49,11 @@
     inverse_all,
     inverse_flat,
     gmat,
-    hmat,
+    spread,
+    hot,
     rest_all,
     rest_flat,
+    far_sem,
     local_sem,
     face_send,
     face_recv,
@@ -94,12 +95,26 @@
     load_n.start()
     load_s.start()
 
+    def loop(count, action):
+        def one(step, carry):
+            action(step)
+            return carry
+
+        lax.fori_loop(1, count, one, 0)
+
+    def each_wide(action):
+        loop(wides, lambda step: action(lax.rem(col + step, wides)))
+
+    def each_sub(action):
+        loop(subs, lambda step: action(lax.rem(row + step, subs)))
+
     barrier = pltpu.get_barrier_semaphore()
-    each_peer(
-        lambda peer, where: pl.semaphore_signal(
-            barrier, inc=1, device_id=where, device_id_type=MESH
-        )
-    )
+
+    def signal(sem, where):
+        pl.semaphore_signal(sem, inc=1, device_id=where, device_id_type=MESH)
+
+    each_sub(lambda other: signal(barrier, (other, col)))
+    each_wide(lambda other: signal(barrier, (row, other)))
 
     basis = basis_in[...].astype(jnp.float32)
     for f in range(4):
@@ -112,11 +127,11 @@
         marks = jnp.where(row_of == p, corner_map[p], marks)
     corner_all[me] = marks
     table = load_table[...]
-    wanted = load_column[...] * 4
-    pattern = lax.broadcasted_iota(jnp.int32, (table.shape[0], rhs), 0)
-    for f in range(4):
-        chosen = (pattern == wanted + f).astype(jnp.float32)
-        load[f] = dot(chosen.T.astype(jnp.bfloat16), table, ((1,), (0,)))
+    target = 4 * lax.broadcasted_iota(jnp.int32, (rhs, table.shape[0]), 0)
+    source = lax.broadcasted_iota(jnp.int32, (rhs, table.shape[0]), 1)
+    for f in range(4):
+        chosen = (source == target + f).astype(jnp.bfloat16)
+        load[f] = dot(chosen, table, ((1,), (0,)))
         face_out[0, f] = load[f]
     inverse_all[col] = inverse_in[...]
     for f in range(4):
@@ -127,7 +142,8 @@
                 face_in[turn, f] = jnp.zeros((rhs, width), jnp.float32)
             basis_near[f] = jnp.zeros((prims, width), jnp.float32)
 
-    pl.semaphore_wait(barrier, devices - 1)
+    pl.semaphore_wait(barrier, subs - 1 + wides - 1)
+    each_sub(lambda other: signal(far_sem, (other, col)))
 
     def face_copy(turn, f):
         return pltpu.make_async_remote_copy(
@@ -202,23 +218,16 @@
             def _():
                 face_wait(turn, f)
 
-    send_faces(0)
     for f in range(4):
 
         @pl.when(has[f])
         def _():
             basis_copy(f).start()
 
+    send_faces(0)
+    each_wide(lambda other: inverse_copy(other).start())
+    pl.semaphore_wait(far_sem, subs - 1)
     each_peer(lambda peer, where: corner_copy(peer, where).start())
-
-    def each_wide(action):
-        def one(step, carry):
-            action(lax.rem(col + step, wides))
-            return carry
-
-        lax.fori_loop(1, wides, one, 0)
-
-    each_wide(lambda other: inverse_copy(other).start())
 
     order_of = [jnp.full((rhs, width), face_order[b], jnp.int32) for b in range(4)]
     held = [[order_of[b] == f for f in range(4)] for b in range(4)]
@@ -238,9 +247,36 @@
         return [pick([held[b][f] for b in range(4)], parts) for f in range(4)]
 
     own_basis = jnp.concatenate([basis_out[f] for f in range(4)], axis=1)
-    own_half = own_basis.astype(jnp.bfloat16)
+    gmat[...] = jnp.zeros(gmat.shape, jnp.float32)
+    gmat[0:prims, :] = own_basis
+    for f in range(4):
+
+        @pl.when(has[f])
+        def _():
+            pltpu.make_async_copy(basis_near.at[f], basis_near.at[f], basis_recv.at[f]).wait()
+
+    for f in range(4):
+        gmat[(f + 1) * prims : (f + 2) * prims, f * width : (f + 1) * width] = basis_near[f]
+    sides = jnp.ones((1, width), jnp.float32)
+    weights = jnp.concatenate([share[f] * sides for f in range(4)], axis=1)
+    shared = (gmat[...] * weights).astype(jnp.bfloat16)
     group = min(devices, 32)
     span = group * prims
+    shifts = (0, -wides, wides, -1, 1)
+
+    def restrict(values):
+        high, low = split(values)
+        parts = dot(shared, high, ((1,), (1,))) + dot(shared, low, ((1,), (1,)))
+        return jnp.concatenate([parts[g * prims : (g + 1) * prims] for g in range(5)], axis=1)
+
+    def mark(part):
+        for g in range(5):
+            for d in range(group):
+                peer = jnp.clip(part * group + d + shifts[g], 0, devices - 1)
+                start = g * span + d * prims
+                corner_flat[start : start + prims, :] = corner_all[peer]
+        lanes = lax.broadcasted_iota(jnp.int32, hot.shape, 1)
+        hot[...] = (corner_flat[:, :1] == lanes).astype(jnp.float32).astype(jnp.bfloat16)
 
     def prepare():
         each_wide(
@@ -250,61 +286,39 @@
         )
         for w in range(wides):
             inverse_flat[w * owned : (w + 1) * owned, :] = inverse_all[w]
-        for f in range(4):
-
-            @pl.when(has[f])
-            def _():
-                pltpu.make_async_copy(
-                    basis_near.at[f], basis_near.at[f], basis_recv.at[f]
-                ).wait()
-
         wait_others(corner_all, corner_recv.at[0])
-        gmat[...] = jnp.zeros(gmat.shape, jnp.float32)
-        gmat[0:prims, :] = own_basis
-        for f in range(4):
-            gmat[(f + 1) * prims : (f + 2) * prims, f * width : (f + 1) * width] = basis_near[f]
         lanes = lax.broadcasted_iota(jnp.int32, (prims, order), 1)
         picks = [marks[:, :1] == lanes]
         for f in range(4):
             peer = jnp.where(has[f], near[f][0] * wides + near[f][1], me)
             picks.append(corner_all[peer][:, :1] == lanes)
-        mine = jnp.concatenate([pick.astype(jnp.float32) for pick in picks], axis=0)
+        mine = jnp.concatenate([chosen.astype(jnp.float32) for chosen in picks], axis=0)
         columns = dot(mine, inverse_flat[...], ((1,), (0,)), HIGHEST)
-        spread = dot(columns.T, gmat[0 : 5 * prims, :], ((1,), (0,)), HIGHEST)
-
-        def one(part):
-            for d in range(group):
-                corner_flat[d * prims : (d + 1) * prims, :] = corner_all[part * group + d]
-            wide_lanes = lax.broadcasted_iota(jnp.int32, (span, order), 1)
-            chosen = (corner_flat[:, :1] == wide_lanes).astype(jnp.float32)
-            hmat[pl.ds(pl.multiple_of(part * span, span), span), :] = dot(
-                chosen, spread, ((1,), (0,)), HIGHEST
-            )
-
+        spread[...] = dot(columns.T, gmat[...], ((1,), (0,)), HIGHEST)
         if devices == group:
-            one(0)
-        else:
-            lax.fori_loop(0, devices // group, lambda part, carry: (one(part), carry)[1], 0)
+            mark(0)
 
     def correct(iteration):
         def one(part):
+            if devices > group:
+                mark(part)
             for d in range(group):
                 rest_flat[d * prims : (d + 1) * prims, :] = rest_all[iteration, part * group + d]
-            return dot(
-                rest_flat[...].T,
-                hmat[pl.ds(pl.multiple_of(part * span, span), span), :],
-                ((1,), (0,)),
-                HIGHEST,
+            turned = rest_flat[...].T
+            lined = jnp.concatenate([turned[g * rhs : (g + 1) * rhs] for g in range(5)], axis=1)
+            high, low = split(lined)
+            return dot(high, hot[...], ((1,), (0,))) + dot(low, hot[...], ((1,), (0,)))
+
+        if devices == group:
+            total = one(0)
+        else:
+            total = lax.fori_loop(
+                0,
+                devices // group,
+                lambda part, total: total + one(part),
+                jnp.zeros((rhs, order), jnp.float32),
             )
-
-        if devices == group:
-            return one(0)
-        return lax.fori_loop(
-            0,
-            devices // group,
-            lambda part, total: total + one(part),
-            jnp.zeros((rhs, 4 * width), jnp.float32),
-        )
+        return dot(total, spread[...], ((1,), (0,)), HIGHEST)
 
     for iteration in range(ITERS):
         first = 2 * iteration
@@ -315,12 +329,12 @@
             for f in range(4):
                 face_out[first, f] = load[f] - local[f]
             send_faces(first)
+        rest_all[iteration, me] = restrict(
+            jnp.concatenate([face_out[first, f] for f in range(4)], axis=1)
+        )
+        each_peer(lambda peer, where: rest_copy(iteration, peer, where).start())
         wait_faces(first)
         weighted = [share[f] * (face_out[first, f] + face_in[first, f]) for f in range(4)]
-        high, low = split(jnp.concatenate(weighted, axis=1))
-        restricted = dot(own_half, high, ((1,), (1,))) + dot(own_half, low, ((1,), (1,)))
-        rest_all[iteration, me] = restricted
-        each_peer(lambda peer, where: rest_copy(iteration, peer, where).start())
         if iteration == 0:
             load_n.wait()
         local = apply_local(weighted, neumann)
@@ -365,6 +379,23 @@
         wait_others(rest_all.at[iteration], rest_send.at[iteration])
 
 
+def expand(load_column, values, out):
+    faces, patterns, width = values.shape
+    rhs = out.shape[1]
+    wanted = lax.broadcasted_iota(jnp.int32, (patterns, rhs), 0) == load_column[...]
+    chosen = wanted.astype(jnp.float32).T.astype(jnp.bfloat16)
+    whole = jnp.concatenate([values[f] for f in range(faces)], axis=1)
+    high, low = split(whole)
+    last = (whole - high.astype(jnp.float32) - low.astype(jnp.float32)).astype(jnp.bfloat16)
+    result = (
+        dot(chosen, high, ((1,), (0,)))
+        + dot(chosen, low, ((1,), (0,)))
+        + dot(chosen, last, ((1,), (0,)))
+    )
+    for f in range(faces):
+        out[f] = result[:, f * width : (f + 1) * width]
+
+
 def body(
     load_table, load_column, face_order, schur, neumann, coarse_basis, corner_map, coarse_inverse
 ):
@@ -384,26 +415,28 @@
     hbm = pl.BlockSpec(memory_space=pl.ANY)
     result = pl.pallas_call(
         functools.partial(kernel, (subs, wides)),
-        out_shape=jax.ShapeDtypeStruct((4, rhs, width), f32),
-        in_specs=[smem, smem, vmem, vmem, vmem, vmem, hbm, hbm],
+        out_shape=jax.ShapeDtypeStruct((4, patterns, width), f32),
+        in_specs=[smem, smem, vmem, vmem, vmem, hbm, hbm],
         out_specs=vmem,
         scratch_shapes=[
             pltpu.VMEM((inner, inner), schur.dtype),
             pltpu.VMEM((inner, inner), neumann.dtype),
-            pltpu.VMEM((4, rhs, width), f32),
-            pltpu.VMEM((4, rhs, width), f32),
-            pltpu.VMEM((2 * ITERS, 4, rhs, width), f32),
-            pltpu.VMEM((2 * ITERS, 4, rhs, width), f32),
+            pltpu.VMEM((4, patterns, width), f32),
+            pltpu.VMEM((4, patterns, width), f32),
+            pltpu.VMEM((2 * ITERS, 4, patterns, width), f32),
+            pltpu.VMEM((2 * ITERS, 4, patterns, width), f32),
             pltpu.VMEM((4, prims, width), f32),
             pltpu.VMEM((4, prims, width), f32),
             pltpu.VMEM((devices, prims, 128), jnp.int32),
-            pltpu.VMEM((group * prims, 128), jnp.int32),
+            pltpu.VMEM((5 * group * prims, 128), jnp.int32),
             pltpu.VMEM((wides, owned, order), f32),
             pltpu.VMEM((order, order), f32),
             pltpu.VMEM((5 * prims, 4 * width), f32),
-            pltpu.VMEM((devices * prims, 4 * width), f32),
-            pltpu.VMEM((ITERS, devices, prims, rhs), f32),
-            pltpu.VMEM((group * prims, rhs), f32),
+            pltpu.VMEM((order, 4 * width), f32),
+            pltpu.VMEM((5 * group * prims, order), jnp.bfloat16),
+            pltpu.VMEM((ITERS, devices, prims, 5 * patterns), f32),
+            pltpu.VMEM((group * prims, 5 * patterns), f32),
+            pltpu.SemaphoreType.REGULAR,
             dma((2,)),
             dma((2 * ITERS, 4)),
             dma((2 * ITERS, 4)),
@@ -421,14 +454,20 @@
     )(
         face_order.reshape(4),
         corner_map.reshape(prims),
-        load_column.reshape(1, rhs),
         load_table.reshape(patterns * 4, width),
         coarse_basis.reshape(prims * 4, width),
         coarse_inverse,
         schur.reshape(inner, inner),
         neumann.reshape(inner, inner),
     )
-    return result.reshape(1, 1, 4, rhs, width)
+    full = pl.pallas_call(
+        expand,
+        out_shape=jax.ShapeDtypeStruct((4, rhs, width), f32),
+        in_specs=[vmem, vmem],
+        out_specs=vmem,
+        name="expand",
+    )(load_column.reshape(1, rhs), result)
+    return full.reshape(1, 1, 4, rhs, width)
 
 
 def solution(mesh):

time: 34.9 us -> 29.3 us (0.84)
  Pallas kernels: 33.1 us -> 29.1 us
  local copies, waits for them, and re-layouts: 1.57 us -> 0 us
    pallas_call x1, Pallas kernels: 33.1 us -> 27.4 us  [body(): pl.pallas_call(functools.partial(kernel, (subs, wides)), out_shape=jax.Sh...]
    pallas_call x0 -> x1, Pallas kernels: none -> 1.68 us  [body(): pl.pallas_call(expand, out_shape=jax.ShapeDtypeStruct((4, rhs, width), f3...]
    unnamed x1 -> x0, local copies, waits for them, and re-layouts: 1.57 us -> none
where the time goes in v2:
time: 29.3 us; the launch traced here: 29.1 us
  Pallas kernels  29.1 us (99%)
    pallas_call x1, Pallas kernels, body(): pl.pallas_call(functools.partial(kernel, (subs, wides)), out_shape=jax.Sh...  27.4 us
    pallas_call x1, Pallas kernels, body(): pl.pallas_call(expand, out_shape=jax.ShapeDtypeStruct((4, rhs, width), f3...  1.68 us

profile of v2, /device:TPU:0, one launch (start us, length us, event | category | flops | bytes accessed | tf_op | source)
XLA Modules:
  0.0 29.1 jit_solution(4893086582927937514)
XLA Ops:
  0.0 27.4 %bddc.1.values = f32[4,16,128]{2,1,0:T(8,128)} custom-call(s32[4]{0:T(128)} %bitcast.12, s32[4]{0:T(128)} %bitcast.13, bf16[64,128]{1,0:T(8,128)(2,1)} %bitcast.10, bf16[16,128]{1,0:T(8,128)(2,1)} %bitcast.11, f32[6,48]{1,0:T(8,128)} %inverse_in.1, bf16[512,512]{1,0:T(8,128)(2,1)} %bitcast.8, bf16[512,512]{1,0:T(8,128)(2,1)} %bitcast.9), custom_call_target="tpu_custom_call" | custom-call | tf_op jit(solution)/shard_map/bddc/pallas_call | solution.py:416
  27.4 1.7 %expand.1 = f32[4,64,128]{2,1,0:T(8,128)} custom-call(s32[1,64]{1,0:T(1,128)} %bitcast.14, f32[4,16,128]{2,1,0:T(8,128)} %bddc.1.values), custom_call_target="tpu_custom_call" | custom-call | tf_op jit(solution)/shard_map/expand/pallas_call | solution.py:463

commit v3 on v2

--- a/solution.py
+++ b/solution.py
@@ -28,14 +28,19 @@
 
 def kernel(
     sizes,
+    face_order_hbm,
+    corner_map_hbm,
+    load_table_hbm,
+    basis_hbm,
+    inverse_hbm,
+    schur_hbm,
+    neumann_hbm,
+    out,
     face_order,
     corner_map,
     load_table,
     basis_in,
     inverse_in,
-    schur_hbm,
-    neumann_hbm,
-    out,
     schur,
     neumann,
     load,
@@ -92,8 +97,20 @@
 
     load_n = pltpu.make_async_copy(neumann_hbm, neumann, local_sem.at[0])
     load_s = pltpu.make_async_copy(schur_hbm, schur, local_sem.at[1])
-    load_n.start()
-    load_s.start()
+
+    pairs = (
+        (face_order_hbm, face_order),
+        (corner_map_hbm, corner_map),
+        (load_table_hbm, load_table),
+        (basis_hbm, basis_in),
+        (inverse_hbm, inverse_in),
+    )
+    small = [
+        pltpu.make_async_copy(source, target, local_sem.at[2 + i])
+        for i, (source, target) in enumerate(pairs)
+    ]
+    for start in small:
+        start.start()
 
     def loop(count, action):
         def one(step, carry):
@@ -116,13 +133,15 @@
     each_sub(lambda other: signal(barrier, (other, col)))
     each_wide(lambda other: signal(barrier, (row, other)))
 
+    for start in small:
+        start.wait()
     basis = basis_in[...].astype(jnp.float32)
     for f in range(4):
         basis_out[f] = jnp.concatenate(
             [basis[4 * p + f : 4 * p + f + 1] for p in range(prims)], axis=0
         )
-    row_of = lax.broadcasted_iota(jnp.int32, (prims, 128), 0)
-    marks = jnp.zeros((prims, 128), jnp.int32)
+    row_of = lax.broadcasted_iota(jnp.int32, (prims, 16), 0)
+    marks = jnp.zeros((prims, 16), jnp.int32)
     for p in range(prims):
         marks = jnp.where(row_of == p, corner_map[p], marks)
     corner_all[me] = marks
@@ -142,6 +161,8 @@
                 face_in[turn, f] = jnp.zeros((rhs, width), jnp.float32)
             basis_near[f] = jnp.zeros((prims, width), jnp.float32)
 
+    load_n.start()
+    load_s.start()
     pl.semaphore_wait(barrier, subs - 1 + wides - 1)
     each_sub(lambda other: signal(far_sem, (other, col)))
 
@@ -411,14 +432,18 @@
     group = min(devices, 32)
     dma = pltpu.SemaphoreType.DMA
     vmem = pl.BlockSpec(memory_space=pltpu.VMEM)
-    smem = pl.BlockSpec(memory_space=pltpu.SMEM)
     hbm = pl.BlockSpec(memory_space=pl.ANY)
     result = pl.pallas_call(
         functools.partial(kernel, (subs, wides)),
         out_shape=jax.ShapeDtypeStruct((4, patterns, width), f32),
-        in_specs=[smem, smem, vmem, vmem, vmem, hbm, hbm],
+        in_specs=[hbm] * 7,
         out_specs=vmem,
         scratch_shapes=[
+            pltpu.SMEM((4,), face_order.dtype),
+            pltpu.SMEM((prims,), corner_map.dtype),
+            pltpu.VMEM((patterns * 4, width), load_table.dtype),
+            pltpu.VMEM((prims * 4, width), coarse_basis.dtype),
+            pltpu.VMEM((owned, order), f32),
             pltpu.VMEM((inner, inner), schur.dtype),
             pltpu.VMEM((inner, inner), neumann.dtype),
             pltpu.VMEM((4, patterns, width), f32),
@@ -427,8 +452,8 @@
             pltpu.VMEM((2 * ITERS, 4, patterns, width), f32),
             pltpu.VMEM((4, prims, width), f32),
             pltpu.VMEM((4, prims, width), f32),
-            pltpu.VMEM((devices, prims, 128), jnp.int32),
-            pltpu.VMEM((5 * group * prims, 128), jnp.int32),
+            pltpu.VMEM((devices, prims, 16), jnp.int32),
+            pltpu.VMEM((5 * group * prims, 16), jnp.int32),
             pltpu.VMEM((wides, owned, order), f32),
             pltpu.VMEM((order, order), f32),
             pltpu.VMEM((5 * prims, 4 * width), f32),
@@ -437,7 +462,7 @@
             pltpu.VMEM((ITERS, devices, prims, 5 * patterns), f32),
             pltpu.VMEM((group * prims, 5 * patterns), f32),
             pltpu.SemaphoreType.REGULAR,
-            dma((2,)),
+            dma((7,)),
             dma((2 * ITERS, 4)),
             dma((2 * ITERS, 4)),
             dma((4,)),

time: 29.3 us -> 28.6 us (0.976)
  Pallas kernels: 29.1 us -> 28.3 us
    pallas_call x1, Pallas kernels: 27.4 us -> 26.7 us  [body(): pl.pallas_call(functools.partial(kernel, (subs, wides)), out_shape=jax.Sh...]
where the time goes in v3:
time: 28.6 us; the launch traced here: 28.4 us
  Pallas kernels  28.3 us (99%)
    pallas_call x1, Pallas kernels, body(): pl.pallas_call(functools.partial(kernel, (subs, wides)), out_shape=jax.Sh...  26.7 us
    pallas_call x1, Pallas kernels, body(): pl.pallas_call(expand, out_shape=jax.ShapeDtypeStruct((4, rhs, width), f3...  1.68 us

profile of v3, /device:TPU:0, one launch (start us, length us, event | category | flops | bytes accessed | tf_op | source)
XLA Modules:
  0.0 28.4 jit_solution(14614534739812694122)
XLA Ops:
  0.0 26.7 %bddc.1.values = f32[4,16,128]{2,1,0:T(8,128)} custom-call(s32[4]{0:T(128)} %bitcast.12, s32[4]{0:T(128)} %bitcast.13, bf16[64,128]{1,0:T(8,128)(2,1)} %bitcast.10, bf16[16,128]{1,0:T(8,128)(2,1)} %bitcast.11, f32[6,48]{1,0:T(8,128)} %inverse_hbm.1, bf16[512,512]{1,0:T(8,128)(2,1)} %bitcast.8, bf16[512,512]{1,0:T(8,128)(2,1)} %bitcast.9), custom_call_target="tpu_custom_call" | custom-call | tf_op jit(solution)/shard_map/bddc/pallas_call | solution.py:436
  26.7 1.7 %expand.1 = f32[4,64,128]{2,1,0:T(8,128)} custom-call(s32[1,64]{1,0:T(1,128)} %bitcast.14, f32[4,16,128]{2,1,0:T(8,128)} %bddc.1.values), custom_call_target="tpu_custom_call" | custom-call | tf_op jit(solution)/shard_map/expand/pallas_call | solution.py:488

commit v4 on v3

--- a/solution.py
+++ b/solution.py
@@ -287,7 +287,8 @@
 
     def restrict(values):
         high, low = split(values)
-        parts = dot(shared, high, ((1,), (1,))) + dot(shared, low, ((1,), (1,)))
+        both = dot(shared, jnp.concatenate([high, low], axis=0), ((1,), (1,)))
+        parts = both[:, :rhs] + both[:, rhs:]
         return jnp.concatenate([parts[g * prims : (g + 1) * prims] for g in range(5)], axis=1)
 
     def mark(part):
@@ -315,7 +316,7 @@
             picks.append(corner_all[peer][:, :1] == lanes)
         mine = jnp.concatenate([chosen.astype(jnp.float32) for chosen in picks], axis=0)
         columns = dot(mine, inverse_flat[...], ((1,), (0,)), HIGHEST)
-        spread[...] = dot(columns.T, gmat[...], ((1,), (0,)), HIGHEST)
+        spread[0], spread[1] = split(dot(columns.T, gmat[...], ((1,), (0,)), HIGHEST))
         if devices == group:
             mark(0)
 
@@ -328,7 +329,8 @@
             turned = rest_flat[...].T
             lined = jnp.concatenate([turned[g * rhs : (g + 1) * rhs] for g in range(5)], axis=1)
             high, low = split(lined)
-            return dot(high, hot[...], ((1,), (0,))) + dot(low, hot[...], ((1,), (0,)))
+            both = dot(jnp.concatenate([high, low], axis=0), hot[...], ((1,), (0,)))
+            return both[:rhs] + both[rhs:]
 
         if devices == group:
             total = one(0)
@@ -339,7 +341,9 @@
                 lambda part, total: total + one(part),
                 jnp.zeros((rhs, order), jnp.float32),
             )
-        return dot(total, spread[...], ((1,), (0,)), HIGHEST)
+        high, low = split(total)
+        both = dot(jnp.concatenate([high, low], axis=0), spread[0], ((1,), (0,)))
+        return both[:rhs] + both[rhs:] + dot(high, spread[1], ((1,), (0,)))
 
     for iteration in range(ITERS):
         first = 2 * iteration
@@ -457,7 +461,7 @@
             pltpu.VMEM((wides, owned, order), f32),
             pltpu.VMEM((order, order), f32),
             pltpu.VMEM((5 * prims, 4 * width), f32),
-            pltpu.VMEM((order, 4 * width), f32),
+            pltpu.VMEM((2, order, 4 * width), jnp.bfloat16),
             pltpu.VMEM((5 * group * prims, order), jnp.bfloat16),
             pltpu.VMEM((ITERS, devices, prims, 5 * patterns), f32),
             pltpu.VMEM((group * prims, 5 * patterns), f32),

time: 28.6 us -> 28.5 us (level)
  no operation moved by 1% of the time
where the time goes in v4:
time: 28.5 us; the launch traced here: 28.3 us
  Pallas kernels  28.3 us (99%)
    pallas_call x1, Pallas kernels, body(): pl.pallas_call(functools.partial(kernel, (subs, wides)), out_shape=jax.Sh...  26.6 us
    pallas_call x1, Pallas kernels, body(): pl.pallas_call(expand, out_shape=jax.ShapeDtypeStruct((4, rhs, width), f3...  1.68 us

profile of v4, /device:TPU:0, one launch (start us, length us, event | category | flops | bytes accessed | tf_op | source)
XLA Modules:
  0.0 28.3 jit_solution(15097455923337430773)
XLA Ops:
  0.0 26.6 %bddc.1.values = f32[4,16,128]{2,1,0:T(8,128)} custom-call(s32[4]{0:T(128)} %bitcast.12, s32[4]{0:T(128)} %bitcast.13, bf16[64,128]{1,0:T(8,128)(2,1)} %bitcast.10, bf16[16,128]{1,0:T(8,128)(2,1)} %bitcast.11, f32[6,48]{1,0:T(8,128)} %inverse_hbm.1, bf16[512,512]{1,0:T(8,128)(2,1)} %bitcast.8, bf16[512,512]{1,0:T(8,128)(2,1)} %bitcast.9), custom_call_target="tpu_custom_call" | custom-call | tf_op jit(solution)/shard_map/bddc/pallas_call | solution.py:440
  26.6 1.7 %expand.1 = f32[4,64,128]{2,1,0:T(8,128)} custom-call(s32[1,64]{1,0:T(1,128)} %bitcast.14, f32[4,16,128]{2,1,0:T(8,128)} %bddc.1.values), custom_call_target="tpu_custom_call" | custom-call | tf_op jit(solution)/shard_map/expand/pallas_call | solution.py:492
